TPU v7x, 512 devices: a whole 4x8x8 slice. The times are simulated.
512 devices in a mesh: ctx: 64 (over x, z, core), head: 8 (over y).
Axes of the slice: x: 4, y: 8, z: 8, core: 2. Of those that a mesh axis runs over, the one named last changes fastest.
Arguments:
- queries: bfloat16 [12288, 4096], P('ctx', 'head'), may hold values from -6 to 6
- key_rows: bfloat16 [12288, 4096], P('ctx', 'head'), may hold values from -6 to 6
- value_rows: bfloat16 [12288, 4096], P('ctx', 'head'), may hold values from -120 to 120
- gate_rows: bfloat16 [12288, 4096], P('ctx', 'head'), may hold values from -8 to 8
- cotangent: bfloat16 [12288, 4096], P('ctx', 'head'), may hold values from -6 to 6
Outputs:
- grad_queries: bfloat16 [12288, 4096], P('ctx', 'head')
- grad_keys: bfloat16 [12288, 4096], P('ctx', 'head')
- grad_values: bfloat16 [12288, 4096], P('ctx', 'head')
- grad_gates: bfloat16 [12288, 4096], P('ctx', 'head')
All inputs are finite; a program needn't handle non-finite values.
Results may differ from a plain program's by a relative error of at most 0.0065.
Values sent between devices are 32-bit elements; how exact they have to be, the bound alone decides.
A program may use at most 64 MiB of HBM per device.

v0:
```python
import jax
import jax.numpy as jnp
from jax import lax
from jax.sharding import PartitionSpec as P

H = 32
DH = 128
EPSILON = 1e-06


def carried_in(part, axis, combine, identity, reverse):
    count = lax.axis_size(axis)
    place = lax.axis_index(axis)
    ahead = count - 1 - place if reverse else place
    gathered = lax.all_gather(part, axis)
    state = jnp.zeros_like(part) + jnp.asarray(identity, part.dtype)

    def one(step, state):
        source = count - 1 - step if reverse else step
        return combine(state, lax.dynamic_index_in_dim(gathered, source, 0, False))

    return lax.fori_loop(0, ahead, one, state)


def silu_slope(x):
    sig = jax.nn.sigmoid(x)
    return sig * (1.0 + x * (1.0 - sig))


def add_states(earlier, later):
    return earlier + later


def per_device(queries, key_rows, value_rows, gate_rows, cotangent):
    rows, width = queries.shape
    heads = width // DH
    full_width = H * DH
    q_float = queries.astype(jnp.float32)
    k_float = key_rows.astype(jnp.float32)
    lifted_q = jax.nn.silu(q_float).astype(jnp.bfloat16).reshape(rows, heads, DH)
    lifted_k = jax.nn.silu(k_float).astype(jnp.bfloat16).reshape(rows, heads, DH)
    values = value_rows.reshape(rows, heads, DH)
    causal = lax.broadcasted_iota(jnp.int32, (rows, rows), 0) >= lax.broadcasted_iota(
        jnp.int32, (rows, rows), 1
    )
    local_state = jnp.einsum("thd,the->hde", lifted_k, values, preferred_element_type=jnp.float32)
    prefix = carried_in(local_state, "ctx", add_states, jnp.zeros_like(local_state), False)
    scores = jnp.einsum("thd,shd->hts", lifted_q, lifted_k, preferred_element_type=jnp.float32)
    weights = jnp.where(causal[None], scores, 0.0).astype(jnp.bfloat16)
    prefix_low = prefix.astype(jnp.bfloat16)
    attended = jnp.einsum("hts,shd->thd", weights, values, preferred_element_type=jnp.float32)
    attended = attended + jnp.einsum(
        "thd,hde->the", lifted_q, prefix_low, preferred_element_type=jnp.float32
    )
    attended = attended.reshape(rows, width)
    sig = jax.nn.sigmoid(gate_rows.astype(jnp.float32))
    grad_out = cotangent.astype(jnp.float32)
    gated = grad_out * sig
    sumsq = lax.psum(jnp.sum(attended * attended, axis=1), "head")
    rms = jnp.sqrt(sumsq / full_width + EPSILON)[:, None]
    normed = attended / rms
    inner = lax.psum(jnp.sum(gated * normed, axis=1), "head")[:, None]
    grad_gates = (grad_out * normed * sig * (1.0 - sig)).astype(jnp.bfloat16)
    d_attn = (
        ((gated - normed * inner / full_width) / rms).astype(jnp.bfloat16).reshape(rows, heads, DH)
    )
    grad_local = jnp.einsum("thd,the->hde", lifted_q, d_attn, preferred_element_type=jnp.float32)
    suffix = carried_in(grad_local, "ctx", add_states, jnp.zeros_like(grad_local), True)
    suffix_low = suffix.astype(jnp.bfloat16)
    d_scores = jnp.einsum("the,she->hts", d_attn, values, preferred_element_type=jnp.float32)
    d_weights = jnp.where(causal[None], d_scores, 0.0).astype(jnp.bfloat16)
    grad_lq = jnp.einsum("hts,shd->thd", d_weights, lifted_k, preferred_element_type=jnp.float32)
    grad_lq = grad_lq + jnp.einsum(
        "the,hde->thd", d_attn, prefix_low, preferred_element_type=jnp.float32
    )
    grad_lk = jnp.einsum("hts,thd->shd", d_weights, lifted_q, preferred_element_type=jnp.float32)
    grad_lk = grad_lk + jnp.einsum(
        "she,hde->shd", values, suffix_low, preferred_element_type=jnp.float32
    )
    grad_v = jnp.einsum("hts,the->she", weights, d_attn, preferred_element_type=jnp.float32)
    grad_v = grad_v + jnp.einsum(
        "shd,hde->she", lifted_k, suffix_low, preferred_element_type=jnp.float32
    )
    grad_queries = (grad_lq.reshape(rows, width) * silu_slope(q_float)).astype(jnp.bfloat16)
    grad_keys = (grad_lk.reshape(rows, width) * silu_slope(k_float)).astype(jnp.bfloat16)
    grad_values = grad_v.reshape(rows, width).astype(jnp.bfloat16)
    return (grad_queries, grad_keys, grad_values, grad_gates)


def solution(mesh):
    in_specs = (
        P("ctx", "head"),
        P("ctx", "head"),
        P("ctx", "head"),
        P("ctx", "head"),
        P("ctx", "head"),
    )
    out_specs = (P("ctx", "head"), P("ctx", "head"), P("ctx", "head"), P("ctx", "head"))
    return jax.shard_map(
        per_device, mesh=mesh, in_specs=in_specs, out_specs=out_specs, check_vma=False
    )
```

profile of v0, /device:TPU:1, one launch (start us, length us, event | category | flops | bytes accessed | tf_op | source)
XLA Modules:
  0.0 394.5 jit_solution(7202193139114948521)
XLA Ops:
  7.2 1.3 fusion.26
  10.2 112.5 %all-gather.5.cloned.1.call-done = f32[256,128,128]{2,1,0:T(8,128)} async-done(((f32[4,128,128]{2,1,0:T(8,128)}), f32[256,128,128]{2,1,0:T(8,128)}) %all-gather.5.cloned.1.call-update) | async-done | bytes 16777232 | tf_op jit(solution)/shard_map/all_gather | solution.py:15
  122.7 1.0 while.22
  122.8 1.0 bitcast_add_fusion.4
  124.1 13.2 %psum.14 = f32[192]{0:T(256)S(1)} all-reduce(f32[192]{0:T(256)S(1)} %get-tuple-element.103), channel_id=1, replica_groups=mesh['ctx'=64,'head'=8] {'head'}, use_global_device_ids=true, to_apply=%region_3.4 | all-reduce | flops 192 | bytes 1536 | tf_op jit(solution)/shard_map/psum | solution.py:59
  137.3 1.3 multiply_reduce_fusion
  138.6 11.5 %psum.15 = f32[192]{0:T(256)S(1)} all-reduce(f32[192]{0:T(256)S(1)} %multiply_reduce_fusion), channel_id=1, replica_groups=mesh['ctx'=64,'head'=8] {'head'}, use_global_device_ids=true, to_apply=%region_5.6 | all-reduce | flops 192 | bytes 1536 | tf_op jit(solution)/shard_map/psum | solution.py:62
  150.0 2.0 fusion.9
  153.8 1.8 fusion.25
  156.3 165.3 %all-gather.7.cloned.1.call-done = f32[256,128,128]{2,1,0:T(8,128)} async-done(((f32[4,128,128]{2,1,0:T(8,128)}), f32[256,128,128]{2,1,0:T(8,128)}) %all-gather.7.cloned.1.call-update) | async-done | bytes 16777232 | tf_op jit(solution)/shard_map/all_gather | solution.py:15
  321.6 64.1 %while.23 = (s32[]{:T(128)}, f32[4,128,128]{2,1,0:T(8,128)S(1)}, s32[]{:T(128)}, f32[64,4,128,128]{3,2,1,0:T(8,128)}, s32[]{:T(128)}, /*index=5*/s32[]{:T(128)}, s32[]{:T(128)}, s32[]{:T(128)}) while((s32[]{:T(128)}, f32[4,128,128]{2,1,0:T(8,128)S(1)}, s32[]{:T(128)}, f32[64,4,128,128]{3,2,1,0:T(8,128)}, s32[]{:T(128)}, /*index=5*/s32[]{:T(128)}, ...), condition=%wide.region_7.8_spmd, body=%wide.region_6.7_spmd.sunk | while | flops 65542 | bytes 786575 | solution.py:22
  321.6 1.0 bitcast_add_fusion.5
  322.7 1.0 bitcast_add_fusion.5
  323.7 1.0 bitcast_add_fusion.5
  329.9 1.0 bitcast_add_fusion.5
  330.9 1.0 bitcast_add_fusion.5
  331.9 1.0 bitcast_add_fusion.5
  339.2 1.0 bitcast_add_fusion.5
  340.2 1.0 bitcast_add_fusion.5
  341.2 1.0 bitcast_add_fusion.5
  349.5 1.0 bitcast_add_fusion.5
  350.5 1.0 bitcast_add_fusion.5
  351.6 1.0 bitcast_add_fusion.5
  358.8 1.0 bitcast_add_fusion.5
  359.8 1.0 bitcast_add_fusion.5
  360.9 1.0 bitcast_add_fusion.5
  369.1 1.0 bitcast_add_fusion.5
  370.2 1.0 bitcast_add_fusion.5
  371.2 1.0 bitcast_add_fusion.5
  378.4 1.0 bitcast_add_fusion.5
  379.5 1.0 bitcast_add_fusion.5
  380.5 1.0 bitcast_add_fusion.5
  (67 shorter events, 47.8 us)
Async XLA Ops:
  7.2 1.4 copy-start
  7.2 379.6 %copy-start.1 = (bf16[192,512]{1,0:T(8,128)(2,1)S(1)}, bf16[192,512]{1,0:T(8,128)(2,1)}, u32[]{:S(2)}) copy-start(bf16[192,512]{1,0:T(8,128)(2,1)} %param.10) | copy-start | bytes 589828
  7.2 115.5 %all-gather.5.cloned.1.call-start = ((), (), s32[]{:S(2)}) async-start(), calls=%async_computation | async-start | bytes 17039360 | tf_op jit(solution)/shard_map/all_gather | solution.py:15
  9.6 312.0 %all-gather.7.cloned.1.call-start = ((), (), s32[]{:S(2)}) async-start(), calls=%async_computation.1 | async-start | bytes 17039360 | tf_op jit(solution)/shard_map/all_gather | solution.py:15
Sparse Core Ops, SparseCore 0:
  11.4 111.3 all-gather.4
  153.1 168.3 all-gather.6
where the time goes:
time: 397 us; the launch traced here: 394 us
  waiting for transfers between devices  278 us (70%)
  other arithmetic  70.8 us (18%)
  blocking collectives  24.7 us (6%)
  between operations  14.2 us (4%)
  matrix products  4.67 us (1%)
    all_gather x2, waiting for transfers between devices, carried_in(): gathered = lax.all_gather(part, axis)  278 us
    add x63, other arithmetic, add_states(): return earlier + later  63.7 us
    psum x1, blocking collectives, per_device(): sumsq = lax.psum(jnp.sum(attended * attended, axis=1), 'head')  13.2 us
    psum x1, blocking collectives, per_device(): inner = lax.psum(jnp.sum(gated * normed, axis=1), 'head')[:, None]  11.5 us
  transfers between devices with their start and end apart: 2, of which 2 were waited for; matrix products, arithmetic and copies ran while one was open for 1% of the time, Pallas kernels for 0%

commit v1 on v0

--- a/solution.py
+++ b/solution.py
@@ -56,7 +56,8 @@
     sig = jax.nn.sigmoid(gate_rows.astype(jnp.float32))
     grad_out = cotangent.astype(jnp.float32)
     gated = grad_out * sig
-    sumsq = lax.psum(jnp.sum(attended * attended, axis=1), "head")
+    m = jnp.sum(attended * attended, axis=1)
+    sumsq = jnp.sum(lax.all_gather(m, "head"), 0)
     rms = jnp.sqrt(sumsq / full_width + EPSILON)[:, None]
     normed = attended / rms
     inner = lax.psum(jnp.sum(gated * normed, axis=1), "head")[:, None]

time: 397 us -> 397 us (level)
    unnamed x0 -> x1, blocking collectives: none -> 13.4 us
    psum x1 -> x0, blocking collectives: 13.2 us -> none  [per_device(): sumsq = lax.psum(jnp.sum(attended * attended, axis=1), 'head')]
where the time goes in v1:
time: 397 us; the launch traced here: 395 us
  waiting for transfers between devices  276 us (70%)
  other arithmetic  70.9 us (18%)
  blocking collectives  24.9 us (6%)
  between operations  14.8 us (4%)
  matrix products  4.65 us (1%)
    all_gather x2, waiting for transfers between devices, carried_in(): gathered = lax.all_gather(part, axis)  276 us
    add x63, other arithmetic, add_states(): return earlier + later  63.7 us
    unnamed x1, blocking collectives  13.4 us
    psum x1, blocking collectives, per_device(): inner = lax.psum(jnp.sum(gated * normed, axis=1), 'head')[:, None]  11.5 us
  transfers between devices with their start and end apart: 2, of which 2 were waited for; matrix products, arithmetic and copies ran while one was open for 1% of the time, Pallas kernels for 0%

profile of v1, /device:TPU:1, one launch (start us, length us, event | category | flops | bytes accessed | tf_op | source)
XLA Modules:
  0.0 395.1 jit_solution(17875943315351818516)
XLA Ops:
  7.2 1.3 fusion.26
  9.6 1.3 dynamic-slice
  12.1 110.6 %all-gather.6.cloned.1.call-done = f32[256,128,128]{2,1,0:T(8,128)} async-done(((f32[4,128,128]{2,1,0:T(8,128)}), f32[256,128,128]{2,1,0:T(8,128)}) %all-gather.6.cloned.1.call-update) | async-done | bytes 16777232 | tf_op jit(solution)/shard_map/all_gather | solution.py:15
  122.7 1.0 while.22
  122.8 1.0 bitcast_add_fusion.4
  124.4 13.4 %all-reduce = f32[1536]{0:T(1024)S(1)} all-reduce(f32[1536]{0:T(1024)S(1)} %dynamic-update-slice), channel_id=3, replica_groups=mesh['ctx'=64,'head'=8] {'head'}, use_global_device_ids=true, to_apply=%add | all-reduce | flops 1536 | bytes 12288
  137.9 1.3 multiply_reduce_fusion
  139.2 11.5 %psum.7 = f32[192]{0:T(256)S(1)} all-reduce(f32[192]{0:T(256)S(1)} %multiply_reduce_fusion), channel_id=1, replica_groups=mesh['ctx'=64,'head'=8] {'head'}, use_global_device_ids=true, to_apply=%region_5.6 | all-reduce | flops 192 | bytes 1536 | tf_op jit(solution)/shard_map/psum | solution.py:63
  150.7 2.0 fusion.9
  154.4 1.8 fusion.25
  156.9 165.3 %all-gather.8.cloned.1.call-done = f32[256,128,128]{2,1,0:T(8,128)} async-done(((f32[4,128,128]{2,1,0:T(8,128)}), f32[256,128,128]{2,1,0:T(8,128)}) %all-gather.8.cloned.1.call-update) | async-done | bytes 16777232 | tf_op jit(solution)/shard_map/all_gather | solution.py:15
  322.2 64.1 %while.23 = (s32[]{:T(128)}, f32[4,128,128]{2,1,0:T(8,128)S(1)}, s32[]{:T(128)}, f32[64,4,128,128]{3,2,1,0:T(8,128)}, s32[]{:T(128)}, /*index=5*/s32[]{:T(128)}, s32[]{:T(128)}, s32[]{:T(128)}) while((s32[]{:T(128)}, f32[4,128,128]{2,1,0:T(8,128)S(1)}, s32[]{:T(128)}, f32[64,4,128,128]{3,2,1,0:T(8,128)}, s32[]{:T(128)}, /*index=5*/s32[]{:T(128)}, ...), condition=%wide.region_7.8_spmd, body=%wide.region_6.7_spmd.sunk | while | flops 65542 | bytes 786575 | solution.py:22
  322.3 1.0 bitcast_add_fusion.5
  323.3 1.0 bitcast_add_fusion.5
  329.5 1.0 bitcast_add_fusion.5
  330.5 1.0 bitcast_add_fusion.5
  331.6 1.0 bitcast_add_fusion.5
  339.8 1.0 bitcast_add_fusion.5
  340.9 1.0 bitcast_add_fusion.5
  341.9 1.0 bitcast_add_fusion.5
  349.1 1.0 bitcast_add_fusion.5
  350.2 1.0 bitcast_add_fusion.5
  351.2 1.0 bitcast_add_fusion.5
  359.5 1.0 bitcast_add_fusion.5
  360.5 1.0 bitcast_add_fusion.5
  361.5 1.0 bitcast_add_fusion.5
  368.8 1.0 bitcast_add_fusion.5
  369.8 1.0 bitcast_add_fusion.5
  370.8 1.0 bitcast_add_fusion.5
  379.1 1.0 bitcast_add_fusion.5
  380.1 1.0 bitcast_add_fusion.5
  381.2 1.0 bitcast_add_fusion.5
  (72 shorter events, 49.2 us)
Async XLA Ops:
  7.2 1.4 copy-start
  7.2 380.3 %copy-start.1 = (bf16[192,512]{1,0:T(8,128)(2,1)S(1)}, bf16[192,512]{1,0:T(8,128)(2,1)}, u32[]{:S(2)}) copy-start(bf16[192,512]{1,0:T(8,128)(2,1)} %param.10) | copy-start | bytes 589828
  7.2 115.5 %all-gather.6.cloned.1.call-start = ((), (), s32[]{:S(2)}) async-start(), calls=%async_computation | async-start | bytes 17039360 | tf_op jit(solution)/shard_map/all_gather | solution.py:15
  9.6 312.6 %all-gather.8.cloned.1.call-start = ((), (), s32[]{:S(2)}) async-start(), calls=%async_computation.1 | async-start | bytes 17039360 | tf_op jit(solution)/shard_map/all_gather | solution.py:15
Sparse Core Ops, SparseCore 0:
  11.4 111.3 all-gather.5
  153.8 168.4 all-gather.7
